TPU v7x, 32 devices: a whole 2x2x4 slice. The times are simulated.
32 devices in a mesh: cuts: 2 (over core), lx: 2 (over x), ly: 8 (over z, y).
Axes of the slice: x: 2, y: 2, z: 4, core: 2. Of those that a mesh axis runs over, the one named last changes fastest.
Arguments:
- disorder: int32 [16, 16, 128], P('lx', 'ly'), may hold values from 0 to 255
- slice_bounds: float32 [12, 2], P('cuts'), may hold values from -1.5 to 1.5
- start: float32 [12, 32, 16, 16, 128], P('cuts', None, 'lx', 'ly'), may hold values from -36 to 36
- ritz: float32 [12, 8, 16, 16, 128], P('cuts', None, 'lx', 'ly'), may hold values from -4 to 4
Outputs:
- block: float32 [12, 32, 16, 16, 128], P('cuts', None, 'lx', 'ly')
- correlations: float32 [12, 16, 32], P('cuts')
All inputs are finite; a program needn't handle non-finite values.
Results may differ from a plain program's by a relative error of at most 0.000096.
Values sent between devices are 32-bit elements; how exact they have to be, the bound alone decides.
A program may use at most 64 MiB of HBM per device.

v0:
```python
import jax
import jax.numpy as jnp
from jax import lax
from jax.sharding import PartitionSpec as P

LEVELS = 256


def passed_along(value, axis, steps):
    count = lax.axis_size(axis)
    first, last = (max(0, -steps), min(count, count - steps))
    return lax.ppermute(value, axis, [(source, source + steps) for source in range(first, last)])


def padded_2(block, sides, width):
    for axis, dim in sides:
        count = lax.axis_size(axis)
        forward = [(i, i + 1) for i in range(count - 1)]
        forward.append((count - 1, 0))
        backward = [(target, source) for source, target in forward]
        low = lax.ppermute(
            lax.slice_in_dim(block, block.shape[dim] - width, None, axis=dim), axis, forward
        )
        high = lax.ppermute(lax.slice_in_dim(block, 0, width, axis=dim), axis, backward)
        block = jnp.concatenate([low, block, high], axis=dim)
    return block


def apply_scaled(field, onsite, centre):
    inner = field[:, 1:-1, 1:-1]
    beside = field[:, 2:, 1:-1] + field[:, :-2, 1:-1]
    beside = beside + field[:, 1:-1, 2:] + field[:, 1:-1, :-2]
    beside = beside + jnp.roll(inner, 1, 3) + jnp.roll(inner, -1, 3)
    return ((onsite[None] - centre) * inner - beside) / 16.0


def on_device(disorder, slice_bounds, start, ritz):
    onsite = 16.5 * (disorder.astype(jnp.float32) / jnp.float32(LEVELS - 1) - 0.5)
    count = start.shape[0]
    width = start.shape[1]
    centre = jnp.repeat((slice_bounds[:, 0] + slice_bounds[:, 1]) / 2.0, width)[:, None, None, None]
    vectors = start.reshape((count * width,) + start.shape[2:])
    lower_edge = passed_along(ritz[-1:], "cuts", 1)
    upper_edge = passed_along(ritz[:1], "cuts", -1)
    lower = jnp.concatenate([lower_edge, ritz[:-1]], 0)
    upper = jnp.concatenate([ritz[1:], upper_edge], 0)

    def filter_step(field):
        padded = padded_2(field, (("lx", 1), ("ly", 2)), 1)
        return apply_scaled(padded, onsite, centre)

    previous = vectors
    current = filter_step(vectors)
    previous, current = (current, 2.0 * filter_step(current) - previous)
    shape = current.shape
    cells = shape[1] * shape[2] * shape[3]
    total = jnp.float32(cells * lax.axis_size("lx") * lax.axis_size("ly"))
    hp = lax.Precision.HIGHEST
    filtered = current.reshape(count, width, cells)
    window = jnp.concatenate([lower, upper], 1).reshape(count, 2 * ritz.shape[1], cells)
    summed = lax.psum(jnp.einsum("src,svc->srv", window, filtered, precision=hp), ("lx", "ly"))
    correlation = summed / total
    cleaned = filtered - jnp.einsum("srv,src->svc", correlation, window, precision=hp)
    gram = lax.psum(jnp.einsum("sac,sbc->sab", cleaned, cleaned, precision=hp), ("lx", "ly"))
    factor = jnp.linalg.cholesky(gram / total)
    result = jax.scipy.linalg.solve_triangular(factor, cleaned, lower=True)
    return (result.reshape((count, width) + shape[1:]), correlation)


def solution(mesh):
    in_specs = (
        P("lx", "ly", None),
        P("cuts", None),
        P("cuts", None, "lx", "ly", None),
        P("cuts", None, "lx", "ly", None),
    )
    out_specs = (P("cuts", None, "lx", "ly", None), P("cuts", None, None))
    return jax.shard_map(
        on_device, mesh=mesh, in_specs=in_specs, out_specs=out_specs, check_vma=False
    )
```

profile of v0, /device:TPU:0, one launch (start us, length us, event | category | flops | bytes accessed | tf_op | source)
XLA Modules:
  0.0 334.0 jit_solution(6009458818156026938)
XLA Ops:
  1.7 3.0 collective-permute-start
  10.5 3.4 %collective-permute-done.1 = f32[192,1,2,128]{3,2,1,0:T(2,128)S(1)} collective-permute-done((f32[192,1,2,128]{3,2,1,0:T(2,128)S(1)}, f32[192,1,2,128]{3,2,1,0:T(2,128)S(1)}, u32[]{:S(2)}, u32[]{:S(2)}) %collective-permute-start.1) | collective-permute-done | bytes 196640 | tf_op jit(solution)/shard_map/ppermute | solution.py:21
  18.1 4.9 %collective-permute-start.2 = (f32[192,10,1,128]{3,2,1,0:T(1,128)S(1)}, f32[192,10,1,128]{3,2,1,0:T(1,128)}, u32[]{:S(2)}, u32[]{:S(2)}) collective-permute-start(f32[192,10,1,128]{3,2,1,0:T(1,128)S(1)} %get-tuple-element.4), channel_id=1, source_target_pairs={{1,0},{2,1},{3,2},{4,3},{5,4},{6,5},{7,6},{0,7},{9,8},{10,9},{11,1... | collective-permute-start | bytes 2949128 | tf_op jit(solution)/shard_map/ppermute | solution.py:24
  23.8 2.1 fusion.23
  26.0 2.1 fusion.24
  28.2 34.1 %collective-permute-done.2 = f32[192,10,1,128]{3,2,1,0:T(1,128)} collective-permute-done((f32[192,10,1,128]{3,2,1,0:T(1,128)S(1)}, f32[192,10,1,128]{3,2,1,0:T(1,128)}, u32[]{:S(2)}, u32[]{:S(2)}) %collective-permute-start.2) | collective-permute-done | bytes 983072 | tf_op jit(solution)/shard_map/ppermute | solution.py:24
  62.3 9.1 %fusion.1 = f32[192,8,2,128]{3,2,1,0:T(2,128)S(1)} fusion(f32[192,8,2,128]{3,2,1,0:T(2,128)S(1)} %bitcast.24, f32[192,10,1,128]{3,2,1,0:T(1,128)} %collective-permute-done.3, f32[192,1,2,128]{3,2,1,0:T(2,128)S(1)} %copy-done.4, f32[192,1,2,128]{3,2,1,0:T(2,128)S(1)} %copy-done.6, f32[192,10,1,128]{3,2,1,0:T(1,128)} %collective-permute-done.2, ...), kind=kLoop, calls=%fused_computation.6 | loop fusion | flops 7471104 | bytes 8659712 | tf_op jit(solution)/shard_map/div | solution.py:34
  73.8 5.6 %collective-permute-done.4 = f32[192,1,2,128]{3,2,1,0:T(2,128)S(1)} collective-permute-done((f32[192,1,2,128]{3,2,1,0:T(2,128)S(1)}, f32[192,1,2,128]{3,2,1,0:T(2,128)S(1)}, u32[]{:S(2)}, u32[]{:S(2)}) %collective-permute-start.4) | collective-permute-done | bytes 196640 | tf_op jit(solution)/shard_map/ppermute | solution.py:24
  79.3 3.0 collective-permute-done.5
  83.3 2.8 fusion.18
  86.1 2.8 collective-permute-start.6
  88.9 2.1 maximum_maximum_fusion
  91.0 2.6 reshape.34
  93.6 2.1 fusion.20
  95.8 2.1 fusion.21
  98.0 33.2 %collective-permute-done.6 = f32[192,10,1,128]{3,2,1,0:T(1,128)} collective-permute-done((f32[192,10,1,128]{3,2,1,0:T(1,128)}, f32[192,10,1,128]{3,2,1,0:T(1,128)}, u32[]{:S(2)}, u32[]{:S(2)}) %collective-permute-start.6) | collective-permute-done | bytes 983072 | tf_op jit(solution)/shard_map/ppermute | solution.py:24
  131.1 10.1 %fusion.4 = f32[192,8,2,128]{3,2,1,0:T(2,128)} fusion(f32[192,8,2,128]{3,2,1,0:T(2,128)S(1)} %fusion.1, f32[192,10,1,128]{3,2,1,0:T(1,128)} %collective-permute-done.7, f32[192,1,2,128]{3,2,1,0:T(2,128)S(1)} %collective-permute-done.4, f32[192,1,2,128]{3,2,1,0:T(2,128)S(1)} %collective-permute-done.5, f32[192,10,1,128]{3,2,1,0:T(1,128)} %collective-permute-done.6, ...), kind=kLoop, calls=%fused_computation.9 | loop fusion | flops 7864320 | bytes 10232576 | tf_op jit(solution)/shard_map/sub | solution.py:54
  141.2 2.6 reshape.33
  145.2 75.1 %psum.14 = f32[6,16,32]{2,1,0:T(8,128)S(1)} all-reduce(f32[6,16,32]{2,1,0:T(8,128)S(1)} %fusion.28), channel_id=1, replica_groups=mesh['cuts'=2,'lx'=2,'ly'=8] {'lx','ly'}, use_global_device_ids=true, to_apply=%region_0.1 | all-reduce | flops 3072 | bytes 24576 | tf_op jit(solution)/shard_map/psum | solution.py:61
  220.4 2.6 convolution_subtract_fusion
  224.5 72.8 %psum.15 = f32[6,32,32]{1,2,0:T(8,128)S(1)} all-reduce(f32[6,32,32]{1,2,0:T(8,128)S(1)} %fusion.29), channel_id=1, replica_groups=mesh['cuts'=2,'lx'=2,'ly'=8] {'lx','ly'}, use_global_device_ids=true, to_apply=%region_1.2 | all-reduce | flops 6144 | bytes 49152 | tf_op jit(solution)/shard_map/psum | solution.py:64
  297.4 17.6 %custom-call.8 = f32[6,32,32]{2,1,0:T(8,128)S(1)} custom-call(f32[6,32,32]{2,1,0:T(8,128)S(1)} %fusion.17), custom_call_target="Cholesky" | custom-call | tf_op jit(solution)/shard_map/jit(cholesky)/cholesky | solution.py:65
  315.2 14.8 %custom-call.9 = f32[6,1,32,32]{2,3,1,0:T(8,128)S(1)} custom-call(f32[6,1,32,32]{3,2,1,0:T(8,128)S(1)} %select_bitcast_fusion), custom_call_target="InvertDiagBlocksLowerTriangular" | custom-call | tf_op jit(solution)/shard_map/jit(_solve_triangular)/vmap()/triangular_solve | solution.py:66
  331.5 2.5 reshape.35
  (57 shorter events, 20.0 us)
Async XLA Ops:
  1.7 8.8 %collective-permute-start = (f32[192,1,2,128]{3,2,1,0:T(2,128)S(1)}, f32[192,1,2,128]{3,2,1,0:T(2,128)S(1)}, u32[]{:S(2)}, u32[]{:S(2)}) collective-permute-start(f32[192,1,2,128]{3,2,1,0:T(2,128)S(1)} %get-tuple-element.17), channel_id=1, source_target_pairs={{8,0},{0,8},{9,1},{1,9},{10,2},{2,10},{11,3},{3,11},{12,4},{4,12},... | collective-permute-start | bytes 589832 | tf_op jit(solution)/shard_map/ppermute | solution.py:24
  4.7 9.1 %collective-permute-start.1 = (f32[192,1,2,128]{3,2,1,0:T(2,128)S(1)}, f32[192,1,2,128]{3,2,1,0:T(2,128)S(1)}, u32[]{:S(2)}, u32[]{:S(2)}) collective-permute-start(f32[192,1,2,128]{3,2,1,0:T(2,128)S(1)} %get-tuple-element.16), channel_id=1, source_target_pairs={{0,8},{8,0},{1,9},{9,1},{2,10},{10,2},{3,11},{11,3},{4,12},{12,4},... | collective-permute-start | bytes 589832 | tf_op jit(solution)/shard_map/ppermute | solution.py:21
  6.3 82.5 %collective-permute-start.8 = (f32[1,8,8,2,128]{4,3,2,1,0:T(2,128)}, f32[1,8,8,2,128]{4,3,2,1,0:T(2,128)}, u32[]{:S(2)}, u32[]{:S(2)}) collective-permute-start(f32[1,8,8,2,128]{4,3,2,1,0:T(2,128)} %get-tuple-element.18), channel_id=1, source_target_pairs={{0,16},{1,17},{2,18},{3,19},{4,20},{5,21},{6,22},{7,23},{8,24},{9,... | collective-permute-start | bytes 196616 | tf_op jit(solution)/shard_map/ppermute | solution.py:12
  8.4 80.5 %collective-permute-start.9 = (f32[1,8,8,2,128]{4,3,2,1,0:T(2,128)}, f32[1,8,8,2,128]{4,3,2,1,0:T(2,128)}, u32[]{:S(2)}, u32[]{:S(2)}) collective-permute-start(f32[1,8,8,2,128]{4,3,2,1,0:T(2,128)} %get-tuple-element.19), channel_id=1, source_target_pairs={{16,0},{17,1},{18,2},{19,3},{20,4},{21,5},{22,6},{23,7},{24,8},{25... | collective-permute-start | bytes 196616 | tf_op jit(solution)/shard_map/ppermute | solution.py:12
  10.5 3.4 %copy-start.3 = (f32[192,1,2,128]{3,2,1,0:T(2,128)}, f32[192,1,2,128]{3,2,1,0:T(2,128)S(1)}, u32[]{:S(2)}) copy-start(f32[192,1,2,128]{3,2,1,0:T(2,128)S(1)} %collective-permute-done) | copy-start | bytes 589828
  13.8 0.7 copy-start.5
  16.5 6.4 %copy-start.10 = (f32[6,2]{0,1:T(2,128)S(1)}, f32[6,2]{0,1:T(2,128)}, u32[]{:S(2)}) copy-start(f32[6,2]{0,1:T(2,128)} %param.5) | copy-start | bytes 148
  16.6 7.3 %copy-start = (f32[6,32,8,2,128]{4,3,2,1,0:T(2,128)S(1)}, f32[6,32,8,2,128]{4,3,2,1,0:T(2,128)}, u32[]{:S(2)}) copy-start(f32[6,32,8,2,128]{4,3,2,1,0:T(2,128)} %param.6) | copy-start | bytes 4718596
  18.1 44.1 %collective-permute-start.2 = (f32[192,10,1,128]{3,2,1,0:T(1,128)S(1)}, f32[192,10,1,128]{3,2,1,0:T(1,128)}, u32[]{:S(2)}, u32[]{:S(2)}) collective-permute-start(f32[192,10,1,128]{3,2,1,0:T(1,128)S(1)} %get-tuple-element.4), channel_id=1, source_target_pairs={{1,0},{2,1},{3,2},{4,3},{5,4},{6,5},{7,6},{0,7},{9,8},{10,9},{11,1... | collective-permute-start | bytes 2949128 | tf_op jit(solution)/shard_map/ppermute | solution.py:24
  23.0 39.3 %collective-permute-start.3 = (f32[192,10,1,128]{3,2,1,0:T(1,128)S(1)}, f32[192,10,1,128]{3,2,1,0:T(1,128)}, u32[]{:S(2)}, u32[]{:S(2)}) collective-permute-start(f32[192,10,1,128]{3,2,1,0:T(1,128)S(1)} %get-tuple-element.5), channel_id=1, source_target_pairs={{0,1},{1,2},{2,3},{3,4},{4,5},{5,6},{6,7},{7,0},{8,9},{9,10},{10,1... | collective-permute-start | bytes 2949128 | tf_op jit(solution)/shard_map/ppermute | solution.py:21
  23.1 39.1 %copy-start.8 = (f32[192]{0:T(256)}, f32[192]{0:T(256)S(1)}, u32[]{:S(2)}) copy-start(f32[192]{0:T(256)S(1)} %sub.40) | copy-start | bytes 2308
  26.0 36.3 %copy-start.4 = (f32[192,1,2,128]{3,2,1,0:T(2,128)S(1)}, f32[192,1,2,128]{3,2,1,0:T(2,128)}, u32[]{:S(2)}) copy-start(f32[192,1,2,128]{3,2,1,0:T(2,128)} %copy-done.3) | copy-start | bytes 589828
  26.0 36.3 %copy-start.6 = (f32[192,1,2,128]{3,2,1,0:T(2,128)S(1)}, f32[192,1,2,128]{3,2,1,0:T(2,128)}, u32[]{:S(2)}) copy-start(f32[192,1,2,128]{3,2,1,0:T(2,128)} %copy-done.5) | copy-start | bytes 589828
  62.3 11.3 %copy-start.2 = (f32[6,8,8,2,128]{4,3,2,1,0:T(2,128)S(1)}, f32[6,8,8,2,128]{4,3,2,1,0:T(2,128)}, u32[]{:S(2)}) copy-start(f32[6,8,8,2,128]{4,3,2,1,0:T(2,128)} %param.7) | copy-start | bytes 1179652
  71.5 7.8 %collective-permute-start.4 = (f32[192,1,2,128]{3,2,1,0:T(2,128)S(1)}, f32[192,1,2,128]{3,2,1,0:T(2,128)S(1)}, u32[]{:S(2)}, u32[]{:S(2)}) collective-permute-start(f32[192,1,2,128]{3,2,1,0:T(2,128)S(1)} %get-tuple-element.11), channel_id=1, source_target_pairs={{8,0},{0,8},{9,1},{1,9},{10,2},{2,10},{11,3},{3,11},{12,4},{4,12},... | collective-permute-start | bytes 589832 | tf_op jit(solution)/shard_map/ppermute | solution.py:24
  73.0 9.4 %collective-permute-start.5 = (f32[192,1,2,128]{3,2,1,0:T(2,128)S(1)}, f32[192,1,2,128]{3,2,1,0:T(2,128)S(1)}, u32[]{:S(2)}, u32[]{:S(2)}) collective-permute-start(f32[192,1,2,128]{3,2,1,0:T(2,128)S(1)} %get-tuple-element.10), channel_id=1, source_target_pairs={{0,8},{8,0},{1,9},{9,1},{2,10},{10,2},{3,11},{11,3},{4,12},{12,4},... | collective-permute-start | bytes 589832 | tf_op jit(solution)/shard_map/ppermute | solution.py:21
  86.1 45.1 %collective-permute-start.6 = (f32[192,10,1,128]{3,2,1,0:T(1,128)}, f32[192,10,1,128]{3,2,1,0:T(1,128)}, u32[]{:S(2)}, u32[]{:S(2)}) collective-permute-start(f32[192,10,1,128]{3,2,1,0:T(1,128)} %get-tuple-element.2), channel_id=1, source_target_pairs={{1,0},{2,1},{3,2},{4,3},{5,4},{6,5},{7,6},{0,7},{9,8},{10,9},{11,1... | collective-permute-start | bytes 2949128 | tf_op jit(solution)/shard_map/ppermute | solution.py:24
  88.9 42.3 %collective-permute-start.7 = (f32[192,10,1,128]{3,2,1,0:T(1,128)}, f32[192,10,1,128]{3,2,1,0:T(1,128)}, u32[]{:S(2)}, u32[]{:S(2)}) collective-permute-start(f32[192,10,1,128]{3,2,1,0:T(1,128)} %get-tuple-element.3), channel_id=1, source_target_pairs={{0,1},{1,2},{2,3},{3,4},{4,5},{5,6},{6,7},{7,0},{8,9},{9,10},{10,1... | collective-permute-start | bytes 2949128 | tf_op jit(solution)/shard_map/ppermute | solution.py:21
  95.8 35.3 %copy-start.9 = (f32[192]{0:T(256)S(1)}, f32[192]{0:T(256)}, u32[]{:S(2)}) copy-start(f32[192]{0:T(256)} %copy-done.8) | copy-start | bytes 2308
  141.2 2.6 copy-start.1
  220.3 2.6 copy-start.7
where the time goes:
time: 335 us; the launch traced here: 334 us
  blocking collectives  148 us (44%)
  waiting for transfers between devices  80 us (24%)
  other arithmetic  57.5 us (17%)
  local copies, waits for them, and re-layouts  24.5 us (7%)
  starting transfers between devices  16.2 us (5%)
  matrix products  6.98 us (2%)
    psum x1, blocking collectives, on_device(): lax.psum(jnp.einsum('src,svc->srv', window, filtered, precision=hp), ('lx...  75.1 us
    ppermute x4, waiting for transfers between devices, padded_2(): lax.ppermute(lax.slice_in_dim(block, 0, width, axis=dim), axis, backward)  73.6 us
    psum x1, blocking collectives, on_device(): lax.psum(jnp.einsum('sac,sbc->sab', cleaned, cleaned, precision=hp), ('lx...  72.8 us
    another operation x4, other arithmetic, on_device(): factor = jnp.linalg.cholesky(gram / total)  17.7 us
    another operation x3, other arithmetic, on_device(): result = jax.scipy.linalg.solve_triangular(factor, cleaned, lower=True)  14.9 us
    ppermute x4, starting transfers between devices, padded_2(): lax.ppermute(lax.slice_in_dim(block, 0, width, axis=dim), axis, backward)  12.2 us
    sub x1, other arithmetic, on_device(): previous, current = (current, 2.0 * filter_step(current) - previous)  10.1 us
    div x1, other arithmetic, apply_scaled(): return ((onsite[None] - centre) * inner - beside) / 16.0  9.07 us
  transfers between devices with their start and end apart: 10, of which 6 were waited for; matrix products, arithmetic and copies ran while one was open for 10% of the time, Pallas kernels for 0%

commit v1 on v0

--- a/solution.py
+++ b/solution.py
@@ -58,7 +58,8 @@
     hp = lax.Precision.HIGHEST
     filtered = current.reshape(count, width, cells)
     window = jnp.concatenate([lower, upper], 1).reshape(count, 2 * ritz.shape[1], cells)
-    summed = lax.psum(jnp.einsum("src,svc->srv", window, filtered, precision=hp), ("lx", "ly"))
+    search_group_here = lambda base_x: lax.psum(lax.psum(base_x, axis_name="ly"), "lx")
+    summed = search_group_here(jnp.einsum("src,svc->srv", window, filtered, precision=hp))
     correlation = summed / total
     cleaned = filtered - jnp.einsum("srv,src->svc", correlation, window, precision=hp)
     gram = lax.psum(jnp.einsum("sac,sbc->sab", cleaned, cleaned, precision=hp), ("lx", "ly"))

time: 335 us -> 304 us (0.907)
  blocking collectives: 148 us -> 117 us
    psum x1 -> x2, blocking collectives: 75.1 us -> 44.6 us  [the longest x1 35.8 us: on_device(): lax.psum(base_x, axis_name='ly')]
  transfers between devices with their start and end apart: 10 -> 10, of which waited for: 6 -> 6; matrix products, arithmetic and copies ran while one was open for 10% -> 11% of each run, Pallas kernels for 0% -> 0%
where the time goes in v1:
time: 304 us; the launch traced here: 303 us
  blocking collectives  117 us (38%)
  waiting for transfers between devices  80 us (26%)
  other arithmetic  57.5 us (19%)
  local copies, waits for them, and re-layouts  24.5 us (8%)
  starting transfers between devices  16.2 us (5%)
  matrix products  6.98 us (2%)
    ppermute x4, waiting for transfers between devices, padded_2(): lax.ppermute(lax.slice_in_dim(block, 0, width, axis=dim), axis, backward)  73.6 us
    psum x1, blocking collectives, on_device(): lax.psum(jnp.einsum('sac,sbc->sab', cleaned, cleaned, precision=hp), ('lx...  72.5 us
    psum x1, blocking collectives, on_device(): lax.psum(base_x, axis_name='ly')  35.8 us
    another operation x4, other arithmetic, on_device(): factor = jnp.linalg.cholesky(gram / total)  17.7 us
    another operation x3, other arithmetic, on_device(): result = jax.scipy.linalg.solve_triangular(factor, cleaned, lower=True)  14.9 us
    ppermute x4, starting transfers between devices, padded_2(): lax.ppermute(lax.slice_in_dim(block, 0, width, axis=dim), axis, backward)  12.2 us
    sub x1, other arithmetic, on_device(): previous, current = (current, 2.0 * filter_step(current) - previous)  10.1 us
    div x1, other arithmetic, apply_scaled(): return ((onsite[None] - centre) * inner - beside) / 16.0  9.07 us
  transfers between devices with their start and end apart: 10, of which 6 were waited for; matrix products, arithmetic and copies ran while one was open for 11% of the time, Pallas kernels for 0%

profile of v1, /device:TPU:0, one launch (start us, length us, event | category | flops | bytes accessed | tf_op | source)
XLA Modules:
  0.0 303.2 jit_solution(9700470494834097760)
XLA Ops:
  1.7 3.0 collective-permute-start
  10.5 3.4 %collective-permute-done.1 = f32[192,1,2,128]{3,2,1,0:T(2,128)S(1)} collective-permute-done((f32[192,1,2,128]{3,2,1,0:T(2,128)S(1)}, f32[192,1,2,128]{3,2,1,0:T(2,128)S(1)}, u32[]{:S(2)}, u32[]{:S(2)}) %collective-permute-start.1) | collective-permute-done | bytes 196640 | tf_op jit(solution)/shard_map/ppermute | solution.py:21
  18.1 4.9 %collective-permute-start.2 = (f32[192,10,1,128]{3,2,1,0:T(1,128)S(1)}, f32[192,10,1,128]{3,2,1,0:T(1,128)}, u32[]{:S(2)}, u32[]{:S(2)}) collective-permute-start(f32[192,10,1,128]{3,2,1,0:T(1,128)S(1)} %get-tuple-element.4), channel_id=1, source_target_pairs={{1,0},{2,1},{3,2},{4,3},{5,4},{6,5},{7,6},{0,7},{9,8},{10,9},{11,1... | collective-permute-start | bytes 2949128 | tf_op jit(solution)/shard_map/ppermute | solution.py:24
  23.8 2.1 fusion.23
  26.0 2.1 fusion.24
  28.2 34.1 %collective-permute-done.2 = f32[192,10,1,128]{3,2,1,0:T(1,128)} collective-permute-done((f32[192,10,1,128]{3,2,1,0:T(1,128)S(1)}, f32[192,10,1,128]{3,2,1,0:T(1,128)}, u32[]{:S(2)}, u32[]{:S(2)}) %collective-permute-start.2) | collective-permute-done | bytes 983072 | tf_op jit(solution)/shard_map/ppermute | solution.py:24
  62.3 9.1 %fusion.1 = f32[192,8,2,128]{3,2,1,0:T(2,128)S(1)} fusion(f32[192,8,2,128]{3,2,1,0:T(2,128)S(1)} %bitcast.24, f32[192,10,1,128]{3,2,1,0:T(1,128)} %collective-permute-done.3, f32[192,1,2,128]{3,2,1,0:T(2,128)S(1)} %copy-done.4, f32[192,1,2,128]{3,2,1,0:T(2,128)S(1)} %copy-done.6, f32[192,10,1,128]{3,2,1,0:T(1,128)} %collective-permute-done.2, ...), kind=kLoop, calls=%fused_computation.6 | loop fusion | flops 7471104 | bytes 8659712 | tf_op jit(solution)/shard_map/div | solution.py:34
  73.8 5.6 %collective-permute-done.4 = f32[192,1,2,128]{3,2,1,0:T(2,128)S(1)} collective-permute-done((f32[192,1,2,128]{3,2,1,0:T(2,128)S(1)}, f32[192,1,2,128]{3,2,1,0:T(2,128)S(1)}, u32[]{:S(2)}, u32[]{:S(2)}) %collective-permute-start.4) | collective-permute-done | bytes 196640 | tf_op jit(solution)/shard_map/ppermute | solution.py:24
  79.3 3.0 %collective-permute-done.5 = f32[192,1,2,128]{3,2,1,0:T(2,128)S(1)} collective-permute-done((f32[192,1,2,128]{3,2,1,0:T(2,128)S(1)}, f32[192,1,2,128]{3,2,1,0:T(2,128)S(1)}, u32[]{:S(2)}, u32[]{:S(2)}) %collective-permute-start.5) | collective-permute-done | bytes 196640 | tf_op jit(solution)/shard_map/ppermute | solution.py:21
  83.3 2.8 fusion.18
  86.1 2.8 collective-permute-start.6
  91.0 2.6 reshape.34
  93.6 2.1 fusion.20
  95.8 2.1 fusion.21
  98.0 33.2 %collective-permute-done.6 = f32[192,10,1,128]{3,2,1,0:T(1,128)} collective-permute-done((f32[192,10,1,128]{3,2,1,0:T(1,128)}, f32[192,10,1,128]{3,2,1,0:T(1,128)}, u32[]{:S(2)}, u32[]{:S(2)}) %collective-permute-start.6) | collective-permute-done | bytes 983072 | tf_op jit(solution)/shard_map/ppermute | solution.py:24
  131.1 10.1 %fusion.4 = f32[192,8,2,128]{3,2,1,0:T(2,128)} fusion(f32[192,8,2,128]{3,2,1,0:T(2,128)S(1)} %fusion.1, f32[192,10,1,128]{3,2,1,0:T(1,128)} %collective-permute-done.7, f32[192,1,2,128]{3,2,1,0:T(2,128)S(1)} %collective-permute-done.4, f32[192,1,2,128]{3,2,1,0:T(2,128)S(1)} %collective-permute-done.5, f32[192,10,1,128]{3,2,1,0:T(1,128)} %collective-permute-done.6, ...), kind=kLoop, calls=%fused_computation.9 | loop fusion | flops 7864320 | bytes 10232576 | tf_op jit(solution)/shard_map/sub | solution.py:54
  141.2 2.6 reshape.33
  145.2 35.8 %psum.21 = f32[6,16,32]{2,1,0:T(8,128)S(1)} all-reduce(f32[6,16,32]{2,1,0:T(8,128)S(1)} %fusion.28), channel_id=1, replica_groups=mesh['cuts'=2,'lx'=2,'ly'=8] {'ly'}, use_global_device_ids=true, to_apply=%region_0.1 | all-reduce | flops 3072 | bytes 24576 | tf_op jit(solution)/shard_map/psum | solution.py:61
  181.0 8.8 %psum.22 = f32[6,16,32]{2,1,0:T(8,128)S(1)} all-reduce(f32[6,16,32]{2,1,0:T(8,128)S(1)} %psum.21), channel_id=1, replica_groups=mesh['cuts'=2,'lx'=2,'ly'=8] {'lx'}, use_global_device_ids=true, to_apply=%region_1.2 | all-reduce | flops 3072 | bytes 24576 | tf_op jit(solution)/shard_map/psum | solution.py:61
  189.9 2.6 convolution_subtract_fusion
  194.0 72.5 %psum.23 = f32[6,32,32]{1,2,0:T(8,128)S(1)} all-reduce(f32[6,32,32]{1,2,0:T(8,128)S(1)} %fusion.29), channel_id=1, replica_groups=mesh['cuts'=2,'lx'=2,'ly'=8] {'lx','ly'}, use_global_device_ids=true, to_apply=%region_2.3 | all-reduce | flops 6144 | bytes 49152 | tf_op jit(solution)/shard_map/psum | solution.py:65
  266.6 17.6 %custom-call.8 = f32[6,32,32]{2,1,0:T(8,128)S(1)} custom-call(f32[6,32,32]{2,1,0:T(8,128)S(1)} %fusion.17), custom_call_target="Cholesky" | custom-call | tf_op jit(solution)/shard_map/jit(cholesky)/cholesky | solution.py:66
  284.4 14.8 %custom-call.9 = f32[6,1,32,32]{2,3,1,0:T(8,128)S(1)} custom-call(f32[6,1,32,32]{3,2,1,0:T(8,128)S(1)} %select_bitcast_fusion), custom_call_target="InvertDiagBlocksLowerTriangular" | custom-call | tf_op jit(solution)/shard_map/jit(_solve_triangular)/vmap()/triangular_solve | solution.py:67
  300.7 2.5 reshape.35
  (58 shorter events, 22.1 us)
Async XLA Ops:
  1.7 8.8 %collective-permute-start = (f32[192,1,2,128]{3,2,1,0:T(2,128)S(1)}, f32[192,1,2,128]{3,2,1,0:T(2,128)S(1)}, u32[]{:S(2)}, u32[]{:S(2)}) collective-permute-start(f32[192,1,2,128]{3,2,1,0:T(2,128)S(1)} %get-tuple-element.17), channel_id=1, source_target_pairs={{8,0},{0,8},{9,1},{1,9},{10,2},{2,10},{11,3},{3,11},{12,4},{4,12},... | collective-permute-start | bytes 589832 | tf_op jit(solution)/shard_map/ppermute | solution.py:24
  4.7 9.1 %collective-permute-start.1 = (f32[192,1,2,128]{3,2,1,0:T(2,128)S(1)}, f32[192,1,2,128]{3,2,1,0:T(2,128)S(1)}, u32[]{:S(2)}, u32[]{:S(2)}) collective-permute-start(f32[192,1,2,128]{3,2,1,0:T(2,128)S(1)} %get-tuple-element.16), channel_id=1, source_target_pairs={{0,8},{8,0},{1,9},{9,1},{2,10},{10,2},{3,11},{11,3},{4,12},{12,4},... | collective-permute-start | bytes 589832 | tf_op jit(solution)/shard_map/ppermute | solution.py:21
  6.3 82.5 %collective-permute-start.8 = (f32[1,8,8,2,128]{4,3,2,1,0:T(2,128)}, f32[1,8,8,2,128]{4,3,2,1,0:T(2,128)}, u32[]{:S(2)}, u32[]{:S(2)}) collective-permute-start(f32[1,8,8,2,128]{4,3,2,1,0:T(2,128)} %get-tuple-element.18), channel_id=1, source_target_pairs={{0,16},{1,17},{2,18},{3,19},{4,20},{5,21},{6,22},{7,23},{8,24},{9,... | collective-permute-start | bytes 196616 | tf_op jit(solution)/shard_map/ppermute | solution.py:12
  8.4 80.5 %collective-permute-start.9 = (f32[1,8,8,2,128]{4,3,2,1,0:T(2,128)}, f32[1,8,8,2,128]{4,3,2,1,0:T(2,128)}, u32[]{:S(2)}, u32[]{:S(2)}) collective-permute-start(f32[1,8,8,2,128]{4,3,2,1,0:T(2,128)} %get-tuple-element.19), channel_id=1, source_target_pairs={{16,0},{17,1},{18,2},{19,3},{20,4},{21,5},{22,6},{23,7},{24,8},{25... | collective-permute-start | bytes 196616 | tf_op jit(solution)/shard_map/ppermute | solution.py:12
  10.5 3.4 %copy-start.3 = (f32[192,1,2,128]{3,2,1,0:T(2,128)}, f32[192,1,2,128]{3,2,1,0:T(2,128)S(1)}, u32[]{:S(2)}) copy-start(f32[192,1,2,128]{3,2,1,0:T(2,128)S(1)} %collective-permute-done) | copy-start | bytes 589828
  13.8 0.7 copy-start.5
  16.5 6.4 %copy-start.10 = (f32[6,2]{0,1:T(2,128)S(1)}, f32[6,2]{0,1:T(2,128)}, u32[]{:S(2)}) copy-start(f32[6,2]{0,1:T(2,128)} %param.5) | copy-start | bytes 148
  16.6 7.3 %copy-start = (f32[6,32,8,2,128]{4,3,2,1,0:T(2,128)S(1)}, f32[6,32,8,2,128]{4,3,2,1,0:T(2,128)}, u32[]{:S(2)}) copy-start(f32[6,32,8,2,128]{4,3,2,1,0:T(2,128)} %param.6) | copy-start | bytes 4718596
  18.1 44.1 %collective-permute-start.2 = (f32[192,10,1,128]{3,2,1,0:T(1,128)S(1)}, f32[192,10,1,128]{3,2,1,0:T(1,128)}, u32[]{:S(2)}, u32[]{:S(2)}) collective-permute-start(f32[192,10,1,128]{3,2,1,0:T(1,128)S(1)} %get-tuple-element.4), channel_id=1, source_target_pairs={{1,0},{2,1},{3,2},{4,3},{5,4},{6,5},{7,6},{0,7},{9,8},{10,9},{11,1... | collective-permute-start | bytes 2949128 | tf_op jit(solution)/shard_map/ppermute | solution.py:24
  23.0 39.3 %collective-permute-start.3 = (f32[192,10,1,128]{3,2,1,0:T(1,128)S(1)}, f32[192,10,1,128]{3,2,1,0:T(1,128)}, u32[]{:S(2)}, u32[]{:S(2)}) collective-permute-start(f32[192,10,1,128]{3,2,1,0:T(1,128)S(1)} %get-tuple-element.5), channel_id=1, source_target_pairs={{0,1},{1,2},{2,3},{3,4},{4,5},{5,6},{6,7},{7,0},{8,9},{9,10},{10,1... | collective-permute-start | bytes 2949128 | tf_op jit(solution)/shard_map/ppermute | solution.py:21
  23.1 39.1 %copy-start.8 = (f32[192]{0:T(256)}, f32[192]{0:T(256)S(1)}, u32[]{:S(2)}) copy-start(f32[192]{0:T(256)S(1)} %sub.40) | copy-start | bytes 2308
  26.0 36.3 %copy-start.4 = (f32[192,1,2,128]{3,2,1,0:T(2,128)S(1)}, f32[192,1,2,128]{3,2,1,0:T(2,128)}, u32[]{:S(2)}) copy-start(f32[192,1,2,128]{3,2,1,0:T(2,128)} %copy-done.3) | copy-start | bytes 589828
  26.0 36.3 %copy-start.6 = (f32[192,1,2,128]{3,2,1,0:T(2,128)S(1)}, f32[192,1,2,128]{3,2,1,0:T(2,128)}, u32[]{:S(2)}) copy-start(f32[192,1,2,128]{3,2,1,0:T(2,128)} %copy-done.5) | copy-start | bytes 589828
  62.3 11.3 %copy-start.2 = (f32[6,8,8,2,128]{4,3,2,1,0:T(2,128)S(1)}, f32[6,8,8,2,128]{4,3,2,1,0:T(2,128)}, u32[]{:S(2)}) copy-start(f32[6,8,8,2,128]{4,3,2,1,0:T(2,128)} %param.7) | copy-start | bytes 1179652
  71.5 7.8 %collective-permute-start.4 = (f32[192,1,2,128]{3,2,1,0:T(2,128)S(1)}, f32[192,1,2,128]{3,2,1,0:T(2,128)S(1)}, u32[]{:S(2)}, u32[]{:S(2)}) collective-permute-start(f32[192,1,2,128]{3,2,1,0:T(2,128)S(1)} %get-tuple-element.11), channel_id=1, source_target_pairs={{8,0},{0,8},{9,1},{1,9},{10,2},{2,10},{11,3},{3,11},{12,4},{4,12},... | collective-permute-start | bytes 589832 | tf_op jit(solution)/shard_map/ppermute | solution.py:24
  73.0 9.4 %collective-permute-start.5 = (f32[192,1,2,128]{3,2,1,0:T(2,128)S(1)}, f32[192,1,2,128]{3,2,1,0:T(2,128)S(1)}, u32[]{:S(2)}, u32[]{:S(2)}) collective-permute-start(f32[192,1,2,128]{3,2,1,0:T(2,128)S(1)} %get-tuple-element.10), channel_id=1, source_target_pairs={{0,8},{8,0},{1,9},{9,1},{2,10},{10,2},{3,11},{11,3},{4,12},{12,4},... | collective-permute-start | bytes 589832 | tf_op jit(solution)/shard_map/ppermute | solution.py:21
  86.1 45.1 %collective-permute-start.6 = (f32[192,10,1,128]{3,2,1,0:T(1,128)}, f32[192,10,1,128]{3,2,1,0:T(1,128)}, u32[]{:S(2)}, u32[]{:S(2)}) collective-permute-start(f32[192,10,1,128]{3,2,1,0:T(1,128)} %get-tuple-element.2), channel_id=1, source_target_pairs={{1,0},{2,1},{3,2},{4,3},{5,4},{6,5},{7,6},{0,7},{9,8},{10,9},{11,1... | collective-permute-start | bytes 2949128 | tf_op jit(solution)/shard_map/ppermute | solution.py:24
  88.9 42.3 %collective-permute-start.7 = (f32[192,10,1,128]{3,2,1,0:T(1,128)}, f32[192,10,1,128]{3,2,1,0:T(1,128)}, u32[]{:S(2)}, u32[]{:S(2)}) collective-permute-start(f32[192,10,1,128]{3,2,1,0:T(1,128)} %get-tuple-element.3), channel_id=1, source_target_pairs={{0,1},{1,2},{2,3},{3,4},{4,5},{5,6},{6,7},{7,0},{8,9},{9,10},{10,1... | collective-permute-start | bytes 2949128 | tf_op jit(solution)/shard_map/ppermute | solution.py:21
  95.8 35.3 %copy-start.9 = (f32[192]{0:T(256)S(1)}, f32[192]{0:T(256)}, u32[]{:S(2)}) copy-start(f32[192]{0:T(256)} %copy-done.8) | copy-start | bytes 2308
  141.2 2.6 copy-start.1
  189.8 2.6 copy-start.7
